TPU v7x, 512 devices: a whole 4x8x8 slice. The times are simulated.
512 devices in a mesh: lang: 16 (over z_lo, y), bulk: 32 (over z_hi, x, core).
Axes of the slice: x: 4, y: 8, z: 8 (z_hi: 4, z_lo: 2; z = z_hi * 2 + z_lo), core: 2. Of those that a mesh axis runs over, the one named last changes fastest.
Arguments:
- sources: bfloat16 [524288, 1024], P(('lang', 'bulk')), may hold values from -24 to 24
- lang_ids: int32 [4096], P(('lang', 'bulk')), may hold values from 0 to 15
- centers: float32 [16, 1024], replicated, may hold values from -3 to 3
- targets: bfloat16 [1024, 1024], P('bulk'), may hold values from -12 to 12
Outputs:
- hubness: float32 [1024], P('bulk')
- source_logsum: float32 [524288], P(('lang', 'bulk'))
- source_match: float32 [524288], P(('lang', 'bulk'))
All inputs are finite; a program needn't handle non-finite values.
Results may differ from a plain program's by a relative error of at most 0.0043.
Values may be sent and summed in bfloat16 or wider, within the bound.
A program may use at most 64 MiB of HBM per device.

v0:
```python
import jax
import jax.numpy as jnp
from jax import lax
from jax.sharding import PartitionSpec as P


def tile_scores(target_piece, centered, temper):
    products = lax.dot_general(
        target_piece, centered, (((1,), (1,)), ((), ())), preferred_element_type=jnp.float32
    )
    return products * temper


def read_update(carried, score_tile, hub_part):
    run_peak, run_weight, run_match = carried
    adjusted = 2.0 * score_tile - hub_part[:, None]
    new_peak = jnp.max(adjusted, axis=0)
    weights = jnp.exp(adjusted - new_peak[None, :])
    factor = jnp.exp(run_peak - new_peak)
    return (
        new_peak,
        run_weight * factor + jnp.sum(weights, axis=0),
        run_match * factor + jnp.sum(weights * score_tile, axis=0),
    )


def per_device(sources, lang_ids, centers, targets):
    source_count, feature_width = sources.shape
    block_count = lang_ids.shape[0]
    lang_count = centers.shape[0]
    temper = feature_width ** (-0.5)
    target_local = targets.shape[0]
    chosen = (lang_ids[:, None] == jnp.arange(lang_count, dtype=jnp.int32)[None, :]).astype(
        jnp.float32
    )
    offsets = jnp.dot(
        chosen, centers, precision=lax.Precision.HIGHEST, preferred_element_type=jnp.float32
    )
    grouped = sources.astype(jnp.float32).reshape(
        block_count, source_count // block_count, feature_width
    )
    centered = (
        (grouped - offsets[:, None, :]).reshape(source_count, feature_width).astype(jnp.bfloat16)
    )
    score_tile = tile_scores(lax.all_gather(targets, "bulk", axis=0, tiled=True), centered, temper)
    tile_peak = jnp.max(score_tile, axis=1)
    tile_weight = jnp.sum(jnp.exp(score_tile - tile_peak[:, None]), axis=1)
    score_tile, tile_peak, tile_weight = (score_tile, tile_peak, tile_weight)
    global_peak = lax.pmax(tile_peak, ("lang", "bulk"))
    global_weight = lax.psum(tile_weight * jnp.exp(tile_peak - global_peak), ("lang", "bulk"))
    hubness = global_peak + jnp.log(global_weight)
    start_state = (
        jnp.full((source_count,), -jnp.inf, jnp.float32),
        jnp.zeros((source_count,), jnp.float32),
        jnp.zeros((source_count,), jnp.float32),
    )
    score_tile = tile_scores(lax.all_gather(targets, "bulk", axis=0, tiled=True), centered, temper)
    final_state = read_update(start_state, score_tile, hubness)
    source_logsum = final_state[0] + jnp.log(final_state[1])
    source_match = final_state[2] / final_state[1]
    own_hub = lax.dynamic_slice_in_dim(hubness, lax.axis_index("bulk") * target_local, target_local)
    return (own_hub, source_logsum, source_match)


def solution(mesh):
    in_specs = (P(("lang", "bulk"), None), P(("lang", "bulk")), P(), P("bulk", None))
    out_specs = (P("bulk"), P(("lang", "bulk")), P(("lang", "bulk")))
    return jax.shard_map(
        per_device, mesh=mesh, in_specs=in_specs, out_specs=out_specs, check_vma=False
    )
```

profile of v0, /device:TPU:1, one launch (start us, length us, event | category | flops | bytes accessed | tf_op | source)
XLA Modules:
  0.0 289.6 jit_solution(16624731422087546585)
XLA Ops:
  7.2 0.0 copy-start
  7.2 0.0 all-gather.2.cloned.1.call-start
  7.2 0.7 all-gather.2.cloned.1.call-update
  7.9 0.1 copy-done
  8.0 0.9 fusion.3
  8.9 2.1 fusion
  11.0 66.6 %all-gather.2.cloned.1.call-done = bf16[1024,1024]{1,0:T(8,128)(2,1)} async-done(((bf16[32,1024]{1,0:T(8,128)(2,1)}), bf16[1024,1024]{1,0:T(8,128)(2,1)}) %all-gather.2.cloned.1.call-update) | async-done | bytes 2097168 | tf_op jit(solution)/shard_map/all_gather | solution.py:45
  77.6 5.9 %multiply_reduce_fusion.1 = (f32[1024]{0:T(1024)S(1)}, f32[1024,1024]{0,1:T(8,128)}) fusion(bf16[1024,1024]{1,0:T(8,128)(2,1)S(1)} %fusion, bf16[1024,1024]{1,0:T(8,128)(2,1)} %all-gather.2.cloned.1.call-done), kind=kOutput, calls=%fused_computation.7 | convolution fusion | flops 2149579776 | bytes 8392704 | tf_op jit(solution)/shard_map/dot_general | solution.py:8
  83.5 95.8 %pmax.7 = f32[1024]{0:T(1024)S(1)} all-reduce(f32[1024]{0:T(1024)S(1)} %get-tuple-element.7), channel_id=1, replica_groups=mesh['lang'=16,'bulk'=32] {'lang','bulk'}, use_global_device_ids=true, to_apply=%region_1.0 | all-reduce | flops 1024 | bytes 8192 | tf_op jit(solution)/shard_map/pmax | solution.py:49
  179.3 3.1 %exponential_reduce_fusion = f32[1024]{0:T(1024)S(1)} fusion(f32[1024,1024]{0,1:T(8,128)} %get-tuple-element.8, f32[1024]{0:T(1024)S(1)} %get-tuple-element.7), kind=kLoop, calls=%fused_computation.2 | loop fusion | flops 3144704 | bytes 4202496 | tf_op jit(solution)/shard_map/reduce_sum | solution.py:47
  182.4 94.4 %psum.7 = f32[1024]{0:T(1024)S(1)} all-reduce(f32[1024]{0:T(1024)S(1)} %exponential_multiply_fusion.1), channel_id=1, replica_groups=mesh['lang'=16,'bulk'=32] {'lang','bulk'}, use_global_device_ids=true, to_apply=%region_3.0 | all-reduce | flops 1024 | bytes 8192 | tf_op jit(solution)/shard_map/psum | solution.py:50
  276.8 0.0 copy-start.1
  276.8 2.8 fusion.1
  279.6 0.6 copy-done.1
  280.2 1.3 multiply_reduce_fusion
  281.5 0.6 dynamic_slice.3
  282.1 0.6 add_divide_fusion
  (2 shorter events, 0.0 us)
Async XLA Ops:
  7.2 0.8 copy-start
  7.2 70.4 %all-gather.2.cloned.1.call-start = ((), (), s32[]{:S(2)}) async-start(), calls=%async_computation | async-start | bytes 2162688 | tf_op jit(solution)/shard_map/all_gather | solution.py:45
  276.8 3.4 %copy-start.1 = (f32[1024,1024]{0,1:T(8,128)S(1)}, f32[1024,1024]{0,1:T(8,128)}, u32[]{:S(2)}) copy-start(f32[1024,1024]{0,1:T(8,128)} %get-tuple-element.8) | copy-start | bytes 12582916
Sparse Core Ops, SparseCore 0:
  11.1 66.4 all-gather.1
where the time goes:
time: 290 us
  blocking collectives  190 us (66%)
  waiting for transfers between devices  67.3 us (23%)
  between operations  14.1 us (5%)
  other arithmetic  9.93 us (3%)
  matrix products  6.74 us (2%)
    pmax x1, blocking collectives, per_device(): global_peak = lax.pmax(tile_peak, ('lang', 'bulk'))  95.8 us
    psum x1, blocking collectives, per_device(): lax.psum(tile_weight * jnp.exp(tile_peak - global_peak), ('lang', 'bulk'))  94.4 us
    all_gather x1, waiting for transfers between devices, per_device(): lax.all_gather(targets, 'bulk', axis=0, tiled=True)  66.6 us
    dot_general x1, matrix products, tile_scores(): lax.dot_general(target_piece, centered, (((1,), (1,)), ((), ())), preferr...  5.89 us
  transfers between devices with their start and end apart: 1, of which 1 were waited for; matrix products, arithmetic and copies ran while one was open for 1% of the time, Pallas kernels for 0%

commit v1 on v0

--- a/solution.py
+++ b/solution.py
@@ -47,7 +47,9 @@
     tile_weight = jnp.sum(jnp.exp(score_tile - tile_peak[:, None]), axis=1)
     score_tile, tile_peak, tile_weight = (score_tile, tile_peak, tile_weight)
     global_peak = lax.pmax(tile_peak, ("lang", "bulk"))
-    global_weight = lax.psum(tile_weight * jnp.exp(tile_peak - global_peak), ("lang", "bulk"))
+    global_weight = jnp.sum(
+        lax.all_gather(tile_weight * jnp.exp(tile_peak - global_peak), ("lang", "bulk")), axis=0
+    )
     hubness = global_peak + jnp.log(global_weight)
     start_state = (
         jnp.full((source_count,), -jnp.inf, jnp.float32),

time: 290 us -> 960 us (3.31)
  waiting for transfers between devices: 67.3 us -> 829 us
  blocking collectives: 190 us -> 95.8 us
    all_gather x0 -> x1, waiting for transfers between devices: none -> 762 us  [per_device(): lax.all_gather(tile_weight * jnp.exp(tile_peak - global_peak), ('lang', '...]
    psum x1 -> x0, blocking collectives: 94.4 us -> none  [per_device(): lax.psum(tile_weight * jnp.exp(tile_peak - global_peak), ('lang', 'bulk'))]
  transfers between devices with their start and end apart: 1 -> 2, of which waited for: 1 -> 2; matrix products, arithmetic and copies ran while one was open for 1% -> 0% of each run, Pallas kernels for 0% -> 0%
where the time goes in v1:
time: 960 us
  waiting for transfers between devices  829 us (86%)
  blocking collectives  95.8 us (10%)
  between operations  14.1 us (1%)
  other arithmetic  10.7 us (1%)
    all_gather x1, waiting for transfers between devices, per_device(): lax.all_gather(tile_weight * jnp.exp(tile_peak - global_peak), ('lang', '...  762 us
    pmax x1, blocking collectives, per_device(): global_peak = lax.pmax(tile_peak, ('lang', 'bulk'))  95.8 us
    all_gather x1, waiting for transfers between devices, per_device(): lax.all_gather(targets, 'bulk', axis=0, tiled=True)  66.6 us
  transfers between devices with their start and end apart: 2, of which 2 were waited for; matrix products, arithmetic and copies ran while one was open for 0% of the time, Pallas kernels for 0%

profile of v1, /device:TPU:1, one launch (start us, length us, event | category | flops | bytes accessed | tf_op | source)
XLA Modules:
  0.0 959.8 jit_solution(7335659766481432970)
XLA Ops:
  7.2 0.0 copy-start
  7.2 0.0 all-gather.4.cloned.1.call-start
  7.2 0.7 all-gather.4.cloned.1.call-update
  7.9 0.0 all-gather.6.cloned.1.call-start
  8.0 0.0 copy-done
  8.0 0.9 fusion.3
  8.9 2.1 fusion
  11.0 66.6 %all-gather.4.cloned.1.call-done = bf16[1024,1024]{1,0:T(8,128)(2,1)} async-done(((bf16[32,1024]{1,0:T(8,128)(2,1)}), bf16[1024,1024]{1,0:T(8,128)(2,1)}) %all-gather.4.cloned.1.call-update) | async-done | bytes 2097168 | tf_op jit(solution)/shard_map/all_gather | solution.py:45
  77.6 5.9 multiply_reduce_fusion.1
  83.5 95.8 %pmax.7 = f32[1024]{0:T(1024)S(1)} all-reduce(f32[1024]{0:T(1024)S(1)} %get-tuple-element.7), channel_id=1, replica_groups=mesh['lang'=16,'bulk'=32] {'lang','bulk'}, use_global_device_ids=true, to_apply=%region_1.0 | all-reduce | flops 1024 | bytes 8192 | tf_op jit(solution)/shard_map/pmax | solution.py:49
  179.3 3.1 exponential_reduce_fusion
  182.4 0.6 exponential_multiply_fusion.1
  183.0 0.0 all-gather.6.cloned.1.call-update
  183.0 762.1 %all-gather.6.cloned.1.call-done = f32[524288]{0:T(1024)} async-done(((f32[1024]{0:T(1024)}), f32[524288]{0:T(1024)}) %all-gather.6.cloned.1.call-update) | async-done | bytes 2097168 | tf_op jit(solution)/shard_map/all_gather | solution.py:51
  945.1 1.7 reshape.14
  946.8 0.1 reduce_sum.37
  947.0 0.0 copy-start.1
  947.0 2.8 fusion.1
  949.8 0.6 copy-done.1
  950.4 1.3 multiply_reduce_fusion
  951.7 0.6 dynamic_slice.3
  952.3 0.6 add_divide_fusion
  (1 shorter events, 0.0 us)
Async XLA Ops:
  7.2 0.8 copy-start
  7.2 70.4 %all-gather.4.cloned.1.call-start = ((), (), s32[]{:S(2)}) async-start(), calls=%async_computation | async-start | bytes 2162688 | tf_op jit(solution)/shard_map/all_gather | solution.py:45
  7.9 937.2 %all-gather.6.cloned.1.call-start = ((), (), s32[]{:S(2)}) async-start(), calls=%async_computation.1 | async-start | bytes 2101248 | tf_op jit(solution)/shard_map/all_gather | solution.py:51
  947.0 3.4 copy-start.1
Sparse Core Ops, SparseCore 0:
  11.1 66.4 all-gather.3
  183.1 761.9 all-gather.5
